TPU v7x, 128 devices: a whole 4x4x4 slice. The times are simulated.
128 devices in a mesh: ang: 8 (over x, core), det: 16 (over z, y).
Axes of the slice: x: 4, y: 4, z: 4, core: 2. Of those that a mesh axis runs over, the one named last changes fastest.
Arguments:
- raw_counts: float32 [256, 128, 4096], P('ang', None, 'det'), may hold values from 0.15 to 0.9
- dark_field: float32 [128, 4096], P(None, 'det'), may hold values from 0 to 0.1
- flat_field: float32 [128, 4096], P(None, 'det'), may hold values from 0.8 to 1.2
- destinations: int32 [32, 1], replicated, may hold values from 0 to 15; in each aligned block of 32 rows (0 to 31, 32 to 63, ...) at most 4 rows name the same one
- band_offsets: int32 [4096], replicated, may hold values from 0 to 4092, as said below
- band_weights: float32 [4, 4096], replicated, may hold values from 0.05 to 0.5
Outputs:
- parallel_slabs: float32 [256, 64, 4, 4096], P('ang', 'det')
Inputs may be any that keep to these rules, and one draw needn't show every extreme that they name: `destinations`: no z-slab owner receives more than 4 row blocks, and some owner receives exactly 4. band_offsets[t] lies between t - 8 and t + 5.
All inputs are finite; a program needn't handle non-finite values.
Results may differ from a plain program's by a relative error of at most 0.0001.
Values sent between devices are 32-bit elements; how exact they have to be, the bound alone decides.
A program may use at most 64 MiB of HBM per device.

v0:
```python
import jax
import jax.numpy as jnp
from jax import lax
from jax.sharding import PartitionSpec as P

RB = 4
SMW = 4
ITERS = 3
HB = 8
BW = 4
MOST = 4
cauchy_scale = 0.2


def with_halo(x, sides, width):
    for axis, dim in sides:
        count, length = (lax.axis_size(axis), x.shape[dim])
        up = [(i, (i + 1) % count) for i in range(count - 1)]
        down = [(j, i) for i, j in up]
        last = lax.slice_in_dim(x, length - width, length, axis=dim)
        leading = lax.slice_in_dim(x, 0, width, axis=dim)
        before = lax.ppermute(last, axis, up)
        after = lax.ppermute(leading, axis, down)
        x = jnp.concatenate([before, x, after], axis=dim)
    return x


def smooth_local(values, first_col, total_cols):
    col_width = values.shape[2]
    padded = with_halo(values, (("det", 2),), SMW)
    summed = padded[:, :, 0:col_width]
    for position in range(1, 2 * SMW + 1):
        summed = summed + padded[:, :, position : position + col_width]
    columns = first_col + jnp.arange(col_width, dtype=jnp.int32)
    counts = jnp.minimum(columns + SMW, total_cols - 1) - jnp.maximum(columns - SMW, 0) + 1
    return summed / counts.astype(jnp.float32)


def band_sum(widened, relative, weights, col_width):
    summed = None
    for shift in range(-HB, HB + 1):
        coeff = jnp.zeros((col_width,), jnp.float32)
        for position in range(BW):
            coeff = coeff + jnp.where(relative == shift - position, weights[position], 0.0)
        term = coeff * widened[..., HB + shift : HB + shift + col_width]
        summed = term if summed is None else summed + term
    return summed


def slot_tables(destinations, owners, most):
    targets = destinations[:, 0]
    block_ids = jnp.arange(targets.shape[0], dtype=jnp.int32)
    same_earlier = (targets[:, None] == targets[None, :]) & (
        block_ids[None, :] < block_ids[:, None]
    )
    slot_rank = jnp.sum(same_earlier.astype(jnp.int32), axis=1)
    owner_ids = jnp.arange(owners, dtype=jnp.int32)
    rank_ids = jnp.arange(most, dtype=jnp.int32)
    matching = (
        (targets[None, None, :] == owner_ids[:, None, None])
        & (slot_rank[None, None, :] == rank_ids[None, :, None])
    ).astype(jnp.int32)
    chosen = jnp.sum(matching * block_ids[None, None, :], axis=2)
    filled = jnp.sum(matching, axis=2)
    return (chosen, filled)


def slot_blocks(values, destinations, owners):
    ang_dev, row_count, col_width = values.shape
    blocks = values.reshape(ang_dev, row_count // RB, RB, col_width)
    chosen, filled = slot_tables(destinations, owners, MOST)
    picked = jnp.take(blocks, chosen.reshape(-1), axis=1).reshape(
        ang_dev, owners, MOST, RB, col_width
    )
    return picked * filled[None, :, :, None, None].astype(jnp.float32)


def body(raw_counts, dark_field, flat_field, destinations, band_offsets, band_weights):
    ang_dev, row_count, col_width = raw_counts.shape
    owners = lax.axis_size("det")
    first_col = lax.axis_index("det") * col_width
    total_cols = col_width * owners
    angles = ang_dev * lax.axis_size("ang")
    projected = -jnp.log((raw_counts - dark_field) / (flat_field - dark_field))
    detail = projected - smooth_local(projected, first_col, total_cols)
    gain_map = lax.psum(jnp.sum(detail, axis=0), "ang") / angles
    for reweight_pass in range(ITERS):
        scaled = (detail - gain_map) / cauchy_scale
        weights = 1.0 / (1.0 + scaled * scaled)
        weighted = jnp.sum(weights * detail, axis=0)
        weight_total = jnp.sum(weights, axis=0)
        total_all, weighted_all = lax.psum((weight_total, weighted), "ang")
        gain_map = weighted_all / total_all
    corrected = projected - gain_map
    picked = slot_blocks(corrected, destinations, owners)
    relative_all = band_offsets - jnp.arange(total_cols, dtype=jnp.int32)
    arrived = lax.all_to_all(picked, "det", split_axis=1, concat_axis=4, tiled=True)
    pad_widths = [(0, 0)] * (arrived.ndim - 1) + [(HB, HB)]
    widened_all = jnp.pad(arrived, pad_widths)
    moved = band_sum(widened_all, relative_all, band_weights, arrived.shape[-1])
    return moved.reshape(ang_dev, MOST, RB, total_cols)


def solution(mesh):
    placed = (P("ang", None, "det"), P(None, "det"), P(None, "det"), P(), P(), P())
    return jax.shard_map(
        body, mesh=mesh, in_specs=placed, out_specs=P("ang", "det", None, None), check_vma=False
    )
```

profile of v0, /device:TPU:6, one launch (start us, length us, event | category | flops | bytes accessed | tf_op | source)
XLA Modules:
  0.0 526.5 jit_solution(13446992526522736455)
XLA Ops:
  6.5 5.5 %copy.19 = f32[32,128,256]{1,0,2:T(8,128)} copy(f32[32,128,256]{2,1,0:T(8,128)} %param.6) | data formatting | bytes 8388608 | tf_op args[0]
  12.3 3.0 log_negate_fusion
  15.3 2.0 copy-done
  17.3 3.5 collective-permute-start
  20.8 1.3 collective-permute-start.1
  22.1 0.5 collective-permute-done
  22.6 4.3 collective-permute-done.1
  26.9 19.3 %fusion.36 = (f32[128,256]{0,1:T(8,128)}, f32[32,128,256]{1,0,2:T(8,128)}) fusion(f32[32,128,256]{1,0,2:T(8,128)} %copy-done, f32[256]{0:T(256)S(1)} %add_convert_fusion, f32[32,128,4]{1,0,2:T(8,128)S(1)} %collective-permute-done.1, f32[32,128,4]{1,0,2:T(8,128)S(1)} %collective-permute-done), kind=kLoop, calls=%fused_computation.112 | loop fusion | flops 19890176 | bytes 8651776 | tf_op jit(solution)/shard_map/reduce_sum | solution.py:86
  46.3 0.2 convert_reduce_fusion
  46.5 61.3 %all-reduce.9.cloned.1.call-done = f32[128,256]{0,1:T(8,128)} async-done(((f32[128,256]{0,1:T(8,128)}), f32[128,256]{0,1:T(8,128)}) %all-reduce.9.cloned.1.call-update) | async-done | bytes 131088 | tf_op jit(solution)/shard_map/psum | solution.py:86
  107.8 0.9 broadcast_multiply_fusion
  108.7 4.8 fusion.29
  113.6 0.2 fusion.33
  114.0 59.1 %all-reduce.15.cloned.1.call-done = (f32[128,256]{0,1:T(8,128)}, f32[128,256]{0,1:T(8,128)}) async-done(((f32[128,256]{0,1:T(8,128)}, f32[128,256]{0,1:T(8,128)}), (f32[128,256]{0,1:T(8,128)}, f32[128,256]{0,1:T(8,128)})) %all-reduce.15.cloned.1.call-update) | async-done | bytes 262160 | tf_op jit(solution)/shard_map/psum | solution.py:92
  173.1 1.0 div.57
  174.1 4.8 fusion.30
  179.0 0.2 all-reduce.11.cloned.1.call-start
  179.2 59.4 %all-reduce.13.cloned.1.call-done = (f32[128,256]{0,1:T(8,128)}, f32[128,256]{0,1:T(8,128)}) async-done(((f32[128,256]{0,1:T(8,128)}, f32[128,256]{0,1:T(8,128)}), (f32[128,256]{0,1:T(8,128)}, f32[128,256]{0,1:T(8,128)})) %all-reduce.13.cloned.1.call-update) | async-done | bytes 262160 | tf_op jit(solution)/shard_map/psum | solution.py:92
  238.6 1.0 div.60
  239.6 4.8 fusion.31
  244.4 0.1 copy.17
  244.6 59.5 %all-reduce.11.cloned.1.call-done = (f32[128,256]{0,1:T(8,128)}, f32[128,256]{0,1:T(8,128)}) async-done(((f32[128,256]{0,1:T(8,128)}, f32[128,256]{0,1:T(8,128)}), (f32[128,256]{0,1:T(8,128)}, f32[128,256]{0,1:T(8,128)})) %all-reduce.11.cloned.1.call-update) | async-done | bytes 262160 | tf_op jit(solution)/shard_map/psum | solution.py:92
  304.1 1.0 div.63
  305.1 5.4 %broadcast_subtract_fusion = f32[32,128,256]{1,0,2:T(8,128)} fusion(f32[128,256]{0,1:T(8,128)S(1)} %div.63, f32[128,256]{0,1:T(8,128)S(1)} %copy.20, f32[32,128,256]{1,0,2:T(8,128)} %copy.19, f32[128,256]{0,1:T(8,128)S(1)} %copy.18), kind=kLoop, calls=%fused_computation.59 | loop fusion | flops 4194304 | bytes 8781824 | tf_op jit(solution)/shard_map/sub | solution.py:94
  310.5 5.6 %copy.21 = f32[32,128,256]{2,0,1:T(8,128)} copy(f32[32,128,256]{1,0,2:T(8,128)} %broadcast_subtract_fusion) | data formatting | bytes 8388608 | tf_op jit(solution)/shard_map/sub | solution.py:94
  316.1 6.7 %gather_fusion = f32[64,32,4,256]{3,1,2,0:T(8,128)} fusion(f32[32,32,4,256]{3,0,2,1:T(8,128)} %bitcast.18, s32[1024]{0:T(1024)S(1)} %pad_clamp_fusion), kind=kCustom, calls=%fused_computation | custom fusion | bytes 16777472 | tf_op jit(solution)/shard_map/jit(_take)/gather | solution.py:72
  322.8 8.9 %select_multiply_fusion = f32[32,16,4,4,256]{4,0,3,2,1:T(8,128)} fusion(f32[32,16,4,4,256]{4,0,3,2,1:T(8,128)} %bitcast.20, f32[16,4]{1,0:T(8,128)S(1)} %copy.23, pred[16,4]{1,0:T(8,128)(4,1)S(1)} %copy.17), kind=kLoop, calls=%fused_computation.22 | loop fusion | flops 4194304 | bytes 16777536 | tf_op jit(solution)/shard_map/mul | solution.py:75
  331.6 7.2 %all-to-all-start = ((f32[32,16,4,4,256]{4,0,3,2,1:T(8,128)}), f32[32,16,4,4,256]{4,0,3,2,1:T(8,128)}, u32[]{:S(2)}, u32[]{:S(2)}) async-start(f32[32,16,4,4,256]{4,0,3,2,1:T(8,128)} %select_multiply_fusion), calls=%async_computation | async-start | bytes 16777216 | tf_op jit(solution)/shard_map/all_to_all | solution.py:97
  339.0 127.9 %all-to-all-done = f32[32,16,4,4,256]{4,0,3,2,1:T(8,128)} async-done(((f32[32,16,4,4,256]{4,0,3,2,1:T(8,128)}), f32[32,16,4,4,256]{4,0,3,2,1:T(8,128)}, u32[]{:S(2)}, u32[]{:S(2)}) %all-to-all-start) | async-done | bytes 8388640 | tf_op jit(solution)/shard_map/all_to_all | solution.py:97
  466.8 4.6 copy.26
  471.5 36.4 %add_bitcast_fusion = f32[32,4,4,4096]{3,0,2,1:T(8,128)} fusion(f32[32,1,4,4,4096]{4,0,3,2,1:T(8,128)S(1)} %bitcast.19, f32[4096]{0:T(1024)S(1)} %get-tuple-element.24, f32[4096]{0:T(1024)S(1)} %get-tuple-element.25, f32[4096]{0:T(1024)S(1)} %get-tuple-element.26, f32[4096]{0:T(1024)S(1)} %get-tuple-element.27, f32[4096]{0:T(1024)S(1)} %get-tuple-element.28, ...), kind=kLoop, calls=%fused_computation.1 | loop fusion | flops 69206016 | bytes 17055744 | tf_op jit(solution)/shard_map/reshape | solution.py:101
  507.8 12.2 %copy.25 = f32[32,4,4,4096]{3,2,1,0:T(4,128)} copy(f32[32,4,4,4096]{3,0,2,1:T(8,128)} %add_bitcast_fusion) | data formatting | bytes 16777216 | tf_op jit(solution)/shard_map/reshape | solution.py:101
  (34 shorter events, 0.8 us)
Async XLA Ops:
  6.5 5.5 %copy-start.1 = (f32[128,256]{1,0:T(8,128)S(1)}, f32[128,256]{1,0:T(8,128)}, u32[]{:S(2)}) copy-start(f32[128,256]{1,0:T(8,128)} %param.7) | copy-start | bytes 393220
  6.5 5.6 %copy-start.2 = (f32[128,256]{1,0:T(8,128)S(1)}, f32[128,256]{1,0:T(8,128)}, u32[]{:S(2)}) copy-start(f32[128,256]{1,0:T(8,128)} %param.8) | copy-start | bytes 393220
  6.5 101.3 %all-reduce.9.cloned.1.call-start = ((), (), s32[]{:S(2)}) async-start(), calls=%async_computation.1 | async-start | bytes 262144 | tf_op jit(solution)/shard_map/psum | solution.py:86
  12.2 9.8 %copy-start.5 = (s32[32,1]{0,1:T(1,128)S(1)}, s32[32,1]{0,1:T(1,128)}, u32[]{:S(2)}) copy-start(s32[32,1]{0,1:T(1,128)} %param.9) | copy-start | bytes 388
  15.3 2.0 copy-start
  17.3 5.4 %collective-permute-start = (f32[32,128,4]{1,0,2:T(8,128)S(1)}, f32[32,128,4]{1,0,2:T(8,128)S(1)}, u32[]{:S(2)}, u32[]{:S(2)}) collective-permute-start(f32[32,128,4]{1,0,2:T(8,128)S(1)} %get-tuple-element.21), channel_id=1, source_target_pairs={{0,1},{1,2},{2,3},{3,4},{4,5},{5,6},{6,7},{7,8},{8,9},{9,10},{10,1... | collective-permute-start | bytes 196616 | tf_op jit(solution)/shard_map/ppermute | solution.py:22
  20.8 6.2 %collective-permute-start.1 = (f32[32,128,4]{1,0,2:T(8,128)S(1)}, f32[32,128,4]{1,0,2:T(8,128)S(1)}, u32[]{:S(2)}, u32[]{:S(2)}) collective-permute-start(f32[32,128,4]{1,0,2:T(8,128)S(1)} %get-tuple-element.22), channel_id=1, source_target_pairs={{1,0},{2,1},{3,2},{4,3},{5,4},{6,5},{7,6},{8,7},{9,8},{10,9},{11,1... | collective-permute-start | bytes 196616 | tf_op jit(solution)/shard_map/ppermute | solution.py:23
  46.2 126.9 %all-reduce.15.cloned.1.call-start = ((), (), s32[]{:S(2)}) async-start(), calls=%async_computation.4 | async-start | bytes 524288 | tf_op jit(solution)/shard_map/psum | solution.py:92
  113.5 125.0 %all-reduce.13.cloned.1.call-start = ((), (), s32[]{:S(2)}) async-start(), calls=%async_computation.3 | async-start | bytes 524288 | tf_op jit(solution)/shard_map/psum | solution.py:92
  179.0 125.1 %all-reduce.11.cloned.1.call-start = ((), (), s32[]{:S(2)}) async-start(), calls=%async_computation.2 | async-start | bytes 524288 | tf_op jit(solution)/shard_map/psum | solution.py:92
  331.6 7.2 %copy-start.3 = (f32[4,4096]{1,0:T(4,128)S(1)}, f32[4,4096]{1,0:T(4,128)}, u32[]{:S(2)}) copy-start(f32[4,4096]{1,0:T(4,128)} %param.11) | copy-start | bytes 196612
  331.6 7.3 %copy-start.4 = (s32[4096]{0:T(1024)S(1)}, s32[4096]{0:T(1024)}, u32[]{:S(2)}) copy-start(s32[4096]{0:T(1024)} %param.10) | copy-start | bytes 49156
  331.6 135.2 %all-to-all-start = ((f32[32,16,4,4,256]{4,0,3,2,1:T(8,128)}), f32[32,16,4,4,256]{4,0,3,2,1:T(8,128)}, u32[]{:S(2)}, u32[]{:S(2)}) async-start(f32[32,16,4,4,256]{4,0,3,2,1:T(8,128)} %select_multiply_fusion), calls=%async_computation | async-start | bytes 16777216 | tf_op jit(solution)/shard_map/all_to_all | solution.py:97
Sparse Core Ops, SparseCore 0:
  46.4 61.4 all-reduce.8
  113.7 59.4 all-reduce.14
  179.1 59.4 all-reduce.12
  244.5 59.5 all-reduce.10
where the time goes:
time: 527 us
  waiting for transfers between devices  372 us (71%)
  other arithmetic  91.8 us (17%)
  local copies, waits for them, and re-layouts  37.1 us (7%)
  between operations  13.3 us (3%)
  starting transfers between devices  12.3 us (2%)
    psum x3, waiting for transfers between devices, body(): total_all, weighted_all = lax.psum((weight_total, weighted), 'ang')  178 us
    all_to_all x1, waiting for transfers between devices, body(): lax.all_to_all(picked, 'det', split_axis=1, concat_axis=4, tiled=True)  128 us
    psum x1, waiting for transfers between devices, body(): gain_map = lax.psum(jnp.sum(detail, axis=0), 'ang') / angles  61.3 us
    reshape x1, other arithmetic, body(): return moved.reshape(ang_dev, MOST, RB, total_cols)  36.4 us
    reduce_sum x1, other arithmetic, body(): gain_map = lax.psum(jnp.sum(detail, axis=0), 'ang') / angles  19.3 us
    reduce_sum x3, other arithmetic, body(): weight_total = jnp.sum(weights, axis=0)  14.4 us
    reshape x1, local copies, waits for them, and re-layouts, body(): return moved.reshape(ang_dev, MOST, RB, total_cols)  12.2 us
  transfers between devices with their start and end apart: 7, of which 7 were waited for; matrix products, arithmetic and copies ran while one was open for 0% of the time, Pallas kernels for 0%

commit v1 on v0

--- a/solution.py
+++ b/solution.py
@@ -83,7 +83,7 @@
     angles = ang_dev * lax.axis_size("ang")
     projected = -jnp.log((raw_counts - dark_field) / (flat_field - dark_field))
     detail = projected - smooth_local(projected, first_col, total_cols)
-    gain_map = lax.psum(jnp.sum(detail, axis=0), "ang") / angles
+    gain_map = jnp.sum(lax.all_gather(jnp.sum(detail, axis=0), "ang"), axis=0) / angles
     for reweight_pass in range(ITERS):
         scaled = (detail - gain_map) / cauchy_scale
         weights = 1.0 / (1.0 + scaled * scaled)

time: 527 us -> 493 us (0.935)
  waiting for transfers between devices: 372 us -> 337 us
    psum x1 -> x0, waiting for transfers between devices: 61.3 us -> none  [body(): gain_map = lax.psum(jnp.sum(detail, axis=0), 'ang') / angles]
    all_gather x0 -> x1, waiting for transfers between devices: none -> 26.3 us  [body(): lax.all_gather(jnp.sum(detail, axis=0), 'ang')]
    reduce_sum x1 -> x2, other arithmetic: 19.3 us -> 19.5 us  [the longest x1 19.3 us: body(): jnp.sum(detail, axis=0)]
where the time goes in v1:
time: 493 us
  waiting for transfers between devices  337 us (68%)
  other arithmetic  91.1 us (18%)
  local copies, waits for them, and re-layouts  38.5 us (8%)
  between operations  13.3 us (3%)
  starting transfers between devices  12.3 us (2%)
    psum x3, waiting for transfers between devices, body(): total_all, weighted_all = lax.psum((weight_total, weighted), 'ang')  178 us
    all_to_all x1, waiting for transfers between devices, body(): lax.all_to_all(picked, 'det', split_axis=1, concat_axis=4, tiled=True)  128 us
    reshape x1, other arithmetic, body(): return moved.reshape(ang_dev, MOST, RB, total_cols)  36.4 us
    all_gather x1, waiting for transfers between devices, body(): lax.all_gather(jnp.sum(detail, axis=0), 'ang')  26.3 us
    reduce_sum x1, other arithmetic, body(): jnp.sum(detail, axis=0)  19.3 us
    reduce_sum x3, other arithmetic, body(): weight_total = jnp.sum(weights, axis=0)  14.4 us
    reshape x1, local copies, waits for them, and re-layouts, body(): return moved.reshape(ang_dev, MOST, RB, total_cols)  12.2 us
  transfers between devices with their start and end apart: 7, of which 7 were waited for; matrix products, arithmetic and copies ran while one was open for 0% of the time, Pallas kernels for 0%

profile of v1, /device:TPU:6, one launch (start us, length us, event | category | flops | bytes accessed | tf_op | source)
XLA Modules:
  0.0 492.6 jit_solution(838104568005989341)
XLA Ops:
  6.5 5.5 %copy.25 = f32[32,128,256]{1,0,2:T(8,128)} copy(f32[32,128,256]{2,1,0:T(8,128)} %param.6) | data formatting | bytes 8388608 | tf_op args[0]
  12.2 3.0 log_negate_fusion
  15.3 2.0 copy-done
  17.2 3.5 collective-permute-start
  20.7 1.3 collective-permute-start.1
  22.1 0.6 collective-permute-done
  22.6 4.3 collective-permute-done.1
  26.9 19.3 %fusion.36 = (f32[128,256]{0,1:T(8,128)}, f32[32,128,256]{1,0,2:T(8,128)}) fusion(f32[32,128,256]{1,0,2:T(8,128)} %copy-done, f32[256]{0:T(256)S(1)} %add_convert_fusion, f32[32,128,4]{1,0,2:T(8,128)S(1)} %collective-permute-done.1, f32[32,128,4]{1,0,2:T(8,128)S(1)} %collective-permute-done), kind=kLoop, calls=%fused_computation.113 | loop fusion | flops 19890176 | bytes 8651776 | tf_op jit(solution)/shard_map/reduce_sum | solution.py:86
  46.3 0.2 convert_reduce_fusion
  46.5 26.3 %all-gather.3.cloned.1.call-done = f32[1024,256]{0,1:T(8,128)} async-done(((f32[128,256]{0,1:T(8,128)}), f32[1024,256]{0,1:T(8,128)}) %all-gather.3.cloned.1.call-update) | async-done | bytes 1048592 | tf_op jit(solution)/shard_map/all_gather | solution.py:86
  72.8 1.4 copy.33
  74.2 0.3 bitcast_reduce_fusion
  74.5 4.8 fusion.29
  79.4 0.2 fusion.33
  79.8 59.4 %all-reduce.12.cloned.1.call-done = (f32[128,256]{0,1:T(8,128)}, f32[128,256]{0,1:T(8,128)}) async-done(((f32[128,256]{0,1:T(8,128)}, f32[128,256]{0,1:T(8,128)}), (f32[128,256]{0,1:T(8,128)}, f32[128,256]{0,1:T(8,128)})) %all-reduce.12.cloned.1.call-update) | async-done | bytes 262160 | tf_op jit(solution)/shard_map/psum | solution.py:92
  139.2 1.0 div.57
  140.2 4.8 fusion.30
  145.0 0.2 all-reduce.8.cloned.1.call-start
  145.2 59.4 %all-reduce.10.cloned.1.call-done = (f32[128,256]{0,1:T(8,128)}, f32[128,256]{0,1:T(8,128)}) async-done(((f32[128,256]{0,1:T(8,128)}, f32[128,256]{0,1:T(8,128)}), (f32[128,256]{0,1:T(8,128)}, f32[128,256]{0,1:T(8,128)})) %all-reduce.10.cloned.1.call-update) | async-done | bytes 262160 | tf_op jit(solution)/shard_map/psum | solution.py:92
  204.6 1.0 div.60
  205.6 4.8 fusion.31
  210.7 59.5 %all-reduce.8.cloned.1.call-done = (f32[128,256]{0,1:T(8,128)}, f32[128,256]{0,1:T(8,128)}) async-done(((f32[128,256]{0,1:T(8,128)}, f32[128,256]{0,1:T(8,128)}), (f32[128,256]{0,1:T(8,128)}, f32[128,256]{0,1:T(8,128)})) %all-reduce.8.cloned.1.call-update) | async-done | bytes 262160 | tf_op jit(solution)/shard_map/psum | solution.py:92
  270.1 1.0 div.63
  271.1 5.4 %broadcast_subtract_fusion = f32[32,128,256]{1,0,2:T(8,128)} fusion(f32[128,256]{0,1:T(8,128)S(1)} %div.63, f32[128,256]{0,1:T(8,128)S(1)} %copy.26, f32[32,128,256]{1,0,2:T(8,128)} %copy.25, f32[128,256]{0,1:T(8,128)S(1)} %copy.24), kind=kLoop, calls=%fused_computation.59 | loop fusion | flops 4194304 | bytes 8781824 | tf_op jit(solution)/shard_map/sub | solution.py:94
  276.5 5.6 %copy.27 = f32[32,128,256]{2,0,1:T(8,128)} copy(f32[32,128,256]{1,0,2:T(8,128)} %broadcast_subtract_fusion) | data formatting | bytes 8388608 | tf_op jit(solution)/shard_map/sub | solution.py:94
  282.1 6.7 %gather_fusion = f32[64,32,4,256]{3,1,2,0:T(8,128)} fusion(f32[32,32,4,256]{3,0,2,1:T(8,128)} %bitcast.23, s32[1024]{0:T(1024)S(1)} %pad_clamp_fusion), kind=kCustom, calls=%fused_computation | custom fusion | bytes 16777472 | tf_op jit(solution)/shard_map/jit(_take)/gather | solution.py:72
  288.8 8.9 %select_multiply_fusion = f32[32,16,4,4,256]{4,0,3,2,1:T(8,128)} fusion(f32[32,16,4,4,256]{4,0,3,2,1:T(8,128)} %bitcast.25, f32[16,4]{1,0:T(8,128)S(1)} %copy.29, pred[16,4]{1,0:T(8,128)(4,1)S(1)} %copy.23), kind=kLoop, calls=%fused_computation.22 | loop fusion | flops 4194304 | bytes 16777536 | tf_op jit(solution)/shard_map/mul | solution.py:75
  297.7 7.2 %all-to-all-start = ((f32[32,16,4,4,256]{4,0,3,2,1:T(8,128)}), f32[32,16,4,4,256]{4,0,3,2,1:T(8,128)}, u32[]{:S(2)}, u32[]{:S(2)}) async-start(f32[32,16,4,4,256]{4,0,3,2,1:T(8,128)} %select_multiply_fusion), calls=%async_computation | async-start | bytes 16777216 | tf_op jit(solution)/shard_map/all_to_all | solution.py:97
  305.0 127.9 %all-to-all-done = f32[32,16,4,4,256]{4,0,3,2,1:T(8,128)} async-done(((f32[32,16,4,4,256]{4,0,3,2,1:T(8,128)}), f32[32,16,4,4,256]{4,0,3,2,1:T(8,128)}, u32[]{:S(2)}, u32[]{:S(2)}) %all-to-all-start) | async-done | bytes 8388640 | tf_op jit(solution)/shard_map/all_to_all | solution.py:97
  432.9 4.6 copy.32
  437.5 36.4 %add_bitcast_fusion = f32[32,4,4,4096]{3,0,2,1:T(8,128)} fusion(f32[32,1,4,4,4096]{4,0,3,2,1:T(8,128)S(1)} %bitcast.24, f32[4096]{0:T(1024)S(1)} %get-tuple-element.24, f32[4096]{0:T(1024)S(1)} %get-tuple-element.25, f32[4096]{0:T(1024)S(1)} %get-tuple-element.26, f32[4096]{0:T(1024)S(1)} %get-tuple-element.27, f32[4096]{0:T(1024)S(1)} %get-tuple-element.28, ...), kind=kLoop, calls=%fused_computation.1 | loop fusion | flops 69206016 | bytes 17055744 | tf_op jit(solution)/shard_map/reshape | solution.py:101
  473.9 12.2 %copy.31 = f32[32,4,4,4096]{3,2,1,0:T(4,128)} copy(f32[32,4,4,4096]{3,0,2,1:T(8,128)} %add_bitcast_fusion) | data formatting | bytes 16777216 | tf_op jit(solution)/shard_map/reshape | solution.py:101
  (36 shorter events, 0.9 us)
Async XLA Ops:
  6.5 5.5 %copy-start.1 = (f32[128,256]{1,0:T(8,128)S(1)}, f32[128,256]{1,0:T(8,128)}, u32[]{:S(2)}) copy-start(f32[128,256]{1,0:T(8,128)} %param.7) | copy-start | bytes 393220
  6.5 5.6 %copy-start.2 = (f32[128,256]{1,0:T(8,128)S(1)}, f32[128,256]{1,0:T(8,128)}, u32[]{:S(2)}) copy-start(f32[128,256]{1,0:T(8,128)} %param.8) | copy-start | bytes 393220
  6.5 66.2 %all-gather.3.cloned.1.call-start = ((), (), s32[]{:S(2)}) async-start(), calls=%async_computation.1 | async-start | bytes 1179648 | tf_op jit(solution)/shard_map/all_gather | solution.py:86
  15.3 2.0 copy-start
  17.2 5.4 %collective-permute-start = (f32[32,128,4]{1,0,2:T(8,128)S(1)}, f32[32,128,4]{1,0,2:T(8,128)S(1)}, u32[]{:S(2)}, u32[]{:S(2)}) collective-permute-start(f32[32,128,4]{1,0,2:T(8,128)S(1)} %get-tuple-element.21), channel_id=1, source_target_pairs={{0,1},{1,2},{2,3},{3,4},{4,5},{5,6},{6,7},{7,8},{8,9},{9,10},{10,1... | collective-permute-start | bytes 196616 | tf_op jit(solution)/shard_map/ppermute | solution.py:22
  20.7 6.2 %collective-permute-start.1 = (f32[32,128,4]{1,0,2:T(8,128)S(1)}, f32[32,128,4]{1,0,2:T(8,128)S(1)}, u32[]{:S(2)}, u32[]{:S(2)}) collective-permute-start(f32[32,128,4]{1,0,2:T(8,128)S(1)} %get-tuple-element.22), channel_id=1, source_target_pairs={{1,0},{2,1},{3,2},{4,3},{5,4},{6,5},{7,6},{8,7},{9,8},{10,9},{11,1... | collective-permute-start | bytes 196616 | tf_op jit(solution)/shard_map/ppermute | solution.py:23
  22.1 24.2 %copy-start.5 = (s32[32,1]{0,1:T(1,128)S(1)}, s32[32,1]{0,1:T(1,128)}, u32[]{:S(2)}) copy-start(s32[32,1]{0,1:T(1,128)} %param.9) | copy-start | bytes 388
  46.2 92.9 %all-reduce.12.cloned.1.call-start = ((), (), s32[]{:S(2)}) async-start(), calls=%async_computation.4 | async-start | bytes 524288 | tf_op jit(solution)/shard_map/psum | solution.py:92
  79.3 125.3 %all-reduce.10.cloned.1.call-start = ((), (), s32[]{:S(2)}) async-start(), calls=%async_computation.3 | async-start | bytes 524288 | tf_op jit(solution)/shard_map/psum | solution.py:92
  145.0 125.1 %all-reduce.8.cloned.1.call-start = ((), (), s32[]{:S(2)}) async-start(), calls=%async_computation.2 | async-start | bytes 524288 | tf_op jit(solution)/shard_map/psum | solution.py:92
  297.7 7.2 %copy-start.3 = (f32[4,4096]{1,0:T(4,128)S(1)}, f32[4,4096]{1,0:T(4,128)}, u32[]{:S(2)}) copy-start(f32[4,4096]{1,0:T(4,128)} %param.11) | copy-start | bytes 196612
  297.7 7.3 %copy-start.4 = (s32[4096]{0:T(1024)S(1)}, s32[4096]{0:T(1024)}, u32[]{:S(2)}) copy-start(s32[4096]{0:T(1024)} %param.10) | copy-start | bytes 49156
  297.7 135.2 %all-to-all-start = ((f32[32,16,4,4,256]{4,0,3,2,1:T(8,128)}), f32[32,16,4,4,256]{4,0,3,2,1:T(8,128)}, u32[]{:S(2)}, u32[]{:S(2)}) async-start(f32[32,16,4,4,256]{4,0,3,2,1:T(8,128)} %select_multiply_fusion), calls=%async_computation | async-start | bytes 16777216 | tf_op jit(solution)/shard_map/all_to_all | solution.py:97
Sparse Core Ops, SparseCore 0:
  46.3 26.3 all-gather.2
  79.4 59.6 all-reduce.11
  145.1 59.4 all-reduce.9
  210.6 59.5 all-reduce.7
